TPU v7x, 128 devices: a whole 4x4x4 slice. The times are simulated.
128 devices in a mesh: dp: 8 (over y, core), ctx: 16 (over z, x).
Axes of the slice: x: 4, y: 4, z: 4, core: 2. Of those that a mesh axis runs over, the one named last changes fastest.
Arguments:
- queries: bfloat16 [8, 4096, 256], P('dp', 'ctx'), may hold values from -6 to 6
- keys: bfloat16 [8, 4096, 256], P('dp', 'ctx'), may hold values from -6 to 6
- values: bfloat16 [8, 4096, 256], P('dp', 'ctx'), may hold values from -6 to 6
- grad_out: bfloat16 [8, 4096, 256], P('dp', 'ctx'), may hold values from -6 to 6
- log_norm: float32 [8, 2, 4096], P('dp', None, 'ctx'), may hold values from 5 to 7
- offsets: int32 [2, 5], replicated, may hold values from 0 to 15
- q_gain: float32 [256], replicated, may hold values from 0.5 to 2
Outputs:
- grad_queries: bfloat16 [8, 4096, 256], P('dp', 'ctx')
- grad_keys: bfloat16 [8, 4096, 256], P('dp', 'ctx')
- grad_values: bfloat16 [8, 4096, 256], P('dp', 'ctx')
- grad_gain: float32 [256], replicated
All inputs are finite; a program needn't handle non-finite values.
Results may differ from a plain program's by a relative error of at most 0.013.
The roundings to bfloat16 on the way count: a program that leaves them out, or rounds other values in their place, can miss the bound.
Values may be sent and summed in bfloat16 or wider, within the bound.
No kernel may reach another device: no remote copies, remote signals or barrier semaphores. Data moves between devices by JAX's collectives and lax.ppermute only.
A program may use at most 64 MiB of HBM per device.

v0:
```python
import math
import jax
import jax.numpy as jnp
from jax import lax
from jax.sharding import PartitionSpec as P

BLOCK = 128
LEVELS = 5


def swapped(block, axis, stride):
    count = lax.axis_size(axis)
    route = []
    for low in range(count):
        high = low | 1 << stride
        if high != low and high < count:
            route += [(low, high), (high, low)]
    return lax.ppermute(block, axis, route)


def slot_table(device_local, offset_vec, stride, block_count):
    slot_count = (block_count + stride - 1) // stride
    base_block = device_local * block_count + jnp.zeros_like(offset_vec)
    first_step = jnp.maximum((base_block - offset_vec + stride - 1) // stride, 0)
    step_index = first_step[..., None] + jnp.arange(slot_count, dtype=jnp.int32)
    global_block = offset_vec[..., None] + stride * step_index
    local_block = global_block - base_block[..., None]
    usable = (step_index < block_count) & (local_block >= 0) & (local_block < block_count)
    return (jnp.clip(local_block, 0, block_count - 1), usable.astype(jnp.float32))


def segment_slots(shift_vec, span_len, block_count):
    device_col = jnp.arange(span_len, dtype=jnp.int32)[:, None]
    seg_block, seg_usable = slot_table(device_col, shift_vec[None, :], span_len, block_count)
    return (seg_block.transpose(1, 0, 2), seg_usable.transpose(1, 0, 2))


def select_table(local_block, block_count):
    return (local_block[..., None] == jnp.arange(block_count, dtype=jnp.int32)).astype(jnp.float32)


def pick_blocks(data, table):
    head_count, block_count = (data.shape[0], data.shape[1])
    flat = data.reshape(head_count, block_count, -1).astype(jnp.float32)
    chosen = jnp.einsum(
        "hsb,hbx->hsx",
        table,
        flat,
        precision=lax.Precision.HIGHEST,
        preferred_element_type=jnp.float32,
    ).astype(data.dtype)
    return chosen.reshape((head_count, -1) + data.shape[3:])


def place_rows(accum, contrib, table, usable):
    head_count, block_count = (accum.shape[0], accum.shape[1])
    slot_count = table.shape[1]
    weights = table * usable[..., None]
    shaped = contrib.reshape(head_count, slot_count, -1)
    added = jnp.einsum(
        "hsb,hsx->hbx",
        weights,
        shaped,
        precision=lax.Precision.HIGHEST,
        preferred_element_type=jnp.float32,
    )
    return accum + added.reshape(accum.shape)


def attend(
    query_rows,
    dout_rows,
    norm_rows,
    query_mask,
    key_rows,
    value_rows,
    key_mask,
    score_scale,
    row_block,
):
    head_count, query_count, head_dim = query_rows.shape
    steps = query_count // row_block

    def split(array):
        return jnp.moveaxis(array.reshape((head_count, steps, row_block) + array.shape[2:]), 1, 0)

    def step_fn(carry, parts):
        query_blk, dout_blk, norm_blk, mask_blk = parts
        scores = (
            jnp.einsum("hqd,hkd->hqk", query_blk, key_rows, preferred_element_type=jnp.float32)
            * score_scale
        )
        probs = jnp.exp(scores - norm_blk[:, :, None]) * mask_blk[:, :, None] * key_mask[:, None, :]
        probs_low = probs.astype(jnp.bfloat16)
        prob_grad = jnp.einsum(
            "hqd,hkd->hqk", dout_blk, value_rows, preferred_element_type=jnp.float32
        )
        dscore = (probs * prob_grad).astype(jnp.bfloat16)
        query_grad = (
            jnp.einsum("hqk,hkd->hqd", dscore, key_rows, preferred_element_type=jnp.float32)
            * score_scale
        )
        key_part = (
            jnp.einsum("hqk,hqd->hkd", dscore, query_blk, preferred_element_type=jnp.float32)
            * score_scale
        )
        value_part = jnp.einsum(
            "hqk,hqd->hkd", probs_low, dout_blk, preferred_element_type=jnp.float32
        )
        return ((carry[0] + key_part, carry[1] + value_part), query_grad)

    start = jnp.zeros((head_count, key_rows.shape[1], head_dim), jnp.float32)
    totals, query_parts = lax.scan(
        step_fn,
        (start, start),
        (split(query_rows), split(dout_rows), split(norm_rows), split(query_mask)),
    )
    query_grad = jnp.moveaxis(query_parts, 0, 1).reshape(head_count, query_count, head_dim)
    return (query_grad, totals[0], totals[1])


def swap_up(payload, my_index, bit_total):
    for bit_idx in range(bit_total):
        partner = swapped(payload, "ctx", bit_idx)
        lower_half = my_index >> bit_idx & 1 == 0
        payload = jnp.where(
            lower_half,
            jnp.concatenate([payload, partner], axis=1),
            jnp.concatenate([partner, payload], axis=1),
        )
    return payload


def swap_down(sums_kv, my_index, bit_total):
    head_count = sums_kv.shape[0]
    for bit_idx in reversed(range(bit_total)):
        halves = sums_kv.reshape(head_count, 2, -1, sums_kv.shape[-1])
        lower_half = my_index >> bit_idx & 1 == 0
        kept_half = jnp.where(lower_half, halves[:, 0], halves[:, 1])
        sent_half = jnp.where(lower_half, halves[:, 1], halves[:, 0])
        sums_kv = kept_half + swapped(sent_half.astype(jnp.bfloat16), "ctx", bit_idx).astype(
            sent_half.dtype
        )
    return sums_kv


def body(queries, keys, values, grad_out, log_norm, offsets, q_gain):
    query_raw = queries[0]
    token_count, proj_width = query_raw.shape
    head_count = log_norm.shape[1]
    head_dim = proj_width // head_count
    block_count = token_count // BLOCK
    ctx_size = lax.axis_size("ctx")
    score_scale = head_dim ** (-0.5)
    scaled = (query_raw.astype(jnp.float32) * q_gain).astype(jnp.bfloat16)

    def heads(matrix):
        return (
            matrix.reshape(token_count, head_count, head_dim)
            .transpose(1, 0, 2)
            .reshape(head_count, block_count, BLOCK, head_dim)
        )

    query_all = heads(scaled)
    key_all = heads(keys[0])
    value_all = heads(values[0])
    dout_all = heads(grad_out[0])
    norm_all = log_norm[0].reshape(head_count, block_count, BLOCK)
    query_acc = jnp.zeros((head_count, block_count, BLOCK, head_dim), jnp.float32)
    kv_acc = jnp.zeros((head_count, block_count, BLOCK, 2 * head_dim), jnp.float32)
    my_index = lax.axis_index("ctx")
    for level_idx in range(LEVELS):
        span_len = min(2**level_idx, ctx_size)
        shift_vec = offsets[:, level_idx] % span_len
        local_block, usable = slot_table(my_index % span_len, shift_vec, span_len, block_count)
        table = select_table(local_block, block_count)
        slot_count = local_block.shape[1]
        row_block = BLOCK * math.gcd(slot_count, max(1, 512 // BLOCK))
        query_own = pick_blocks(query_all, table)
        dout_own = pick_blocks(dout_all, table)
        norm_own = pick_blocks(norm_all, table)
        mask_own = jnp.repeat(usable, BLOCK, axis=1)
        payload = jnp.concatenate(
            [pick_blocks(key_all, table), pick_blocks(value_all, table)], axis=2
        )
        bit_total = span_len.bit_length() - 1
        payload = swap_up(payload, my_index, bit_total)
        seg_block, seg_usable = segment_slots(shift_vec, span_len, block_count)
        seg_mask = jnp.repeat(seg_usable.reshape(head_count, -1), BLOCK, axis=1)
        level_query, level_key, level_value = attend(
            query_own,
            dout_own,
            norm_own,
            mask_own,
            payload[..., :head_dim],
            payload[..., head_dim:],
            seg_mask,
            score_scale,
            row_block,
        )
        sums_kv = jnp.concatenate([level_key, level_value], axis=2)
        sums_kv = swap_down(sums_kv, my_index, bit_total)
        query_acc = place_rows(query_acc, level_query, table, usable)
        kv_acc = place_rows(kv_acc, sums_kv, table, usable)

    def to_rows(field_acc):
        return (
            field_acc.reshape(head_count, token_count, -1)
            .transpose(1, 0, 2)
            .reshape(token_count, -1)
        )

    dq_rows = to_rows(query_acc)
    grad_queries = (dq_rows * q_gain).astype(jnp.bfloat16)
    grad_keys = to_rows(kv_acc[..., :head_dim]).astype(jnp.bfloat16)
    grad_values = to_rows(kv_acc[..., head_dim:]).astype(jnp.bfloat16)
    gain_total = lax.psum(jnp.sum(query_raw.astype(jnp.float32) * dq_rows, axis=0), ("dp", "ctx"))
    return (grad_queries[None], grad_keys[None], grad_values[None], gain_total)


def solution(mesh):
    in_specs = (
        P("dp", "ctx", None),
        P("dp", "ctx", None),
        P("dp", "ctx", None),
        P("dp", "ctx", None),
        P("dp", None, "ctx"),
        P(),
        P(),
    )
    out_specs = (P("dp", "ctx", None), P("dp", "ctx", None), P("dp", "ctx", None), P())
    return jax.shard_map(body, mesh=mesh, in_specs=in_specs, out_specs=out_specs, check_vma=False)
```

profile of v0, /device:TPU:0, one launch (start us, length us, event | category | flops | bytes accessed | tf_op | source)
XLA Modules:
  0.0 272.5 jit_solution(3529592541120777040)
XLA Ops:
  1.7 1.7 clamp_reduce_fusion.3
  34.6 3.2 %collective-permute-start.2 = (bf16[2,256,256]{2,1,0:T(8,128)(2,1)S(1)}, bf16[2,256,256]{2,1,0:T(8,128)(2,1)S(1)}, u32[]{:S(2)}, u32[]{:S(2)}) collective-permute-start(bf16[2,256,256]{2,1,0:T(8,128)(2,1)S(1)} %maximum_select_fusion.7), channel_id=1, source_target_pairs={{0,2},{2,0},{1,3},{3,1},{4,6},{6,4},{5,7},{7,5},{8,10},{10,8},{9,1... | collective-permute-start | bytes 786440 | tf_op jit(solution)/shard_map/ppermute | solution.py:18
  40.1 2.0 collective-permute-start.7
  47.9 9.2 %collective-permute-done.4 = bf16[2,256,256]{2,1,0:T(8,128)(2,1)} collective-permute-done((bf16[2,256,256]{2,1,0:T(8,128)(2,1)}, bf16[2,256,256]{2,1,0:T(8,128)(2,1)}, u32[]{:S(2)}, u32[]{:S(2)}) %collective-permute-start.4) | collective-permute-done | bytes 262176 | tf_op jit(solution)/shard_map/ppermute | solution.py:18
  58.4 2.4 collective-permute-start.5
  63.1 3.0 %collective-permute-start.11 = (bf16[2,256,256]{2,1,0:T(8,128)(2,1)}, bf16[2,256,256]{2,1,0:T(8,128)(2,1)}, u32[]{:S(2)}, u32[]{:S(2)}) collective-permute-start(bf16[2,256,256]{2,1,0:T(8,128)(2,1)} %fusion.49), channel_id=1, source_target_pairs={{0,2},{2,0},{1,3},{3,1},{4,6},{6,4},{5,7},{7,5},{8,10},{10,8},{9,1... | collective-permute-start | bytes 786440 | tf_op jit(solution)/shard_map/ppermute | solution.py:18
  66.1 2.2 maximum_select_fusion.5
  68.4 4.8 %collective-permute-done.5 = bf16[2,512,256]{2,1,0:T(8,128)(2,1)} collective-permute-done((bf16[2,512,256]{2,1,0:T(8,128)(2,1)S(1)}, bf16[2,512,256]{2,1,0:T(8,128)(2,1)}, u32[]{:S(2)}, u32[]{:S(2)}) %collective-permute-start.5) | collective-permute-done | bytes 524320 | tf_op jit(solution)/shard_map/ppermute | solution.py:18
  78.5 3.0 %reshape.1673 = f32[2,2,512,256]{2,1,3,0:T(2,128)S(1)} reshape(f32[2,1024,256]{1,2,0:T(8,128)} %pad_maximum_fusion.1) | data formatting | bytes 4194304 | tf_op jit(solution)/shard_map/reshape | solution.py:137
  81.6 2.9 %fusion.212 = (f32[2,1,512,256]{2,1,3,0:T(1,128)}, f32[2,1,512,256]{2,1,3,0:T(1,128)}) fusion(f32[2,2,512,256]{2,1,3,0:T(2,128)S(1)} %reshape.1673), kind=kLoop, calls=%fused_computation.413 | loop fusion | bytes 4194304 | tf_op jit(solution)/shard_map/slice | solution.py:139
  84.5 2.3 copy.151
  86.9 2.4 copy.152
  89.4 2.7 collective-permute-start.13
  92.1 1.8 maximum_select_fusion.2
  93.8 3.7 %collective-permute-start.9 = (bf16[2,1024,256]{2,1,0:T(8,128)(2,1)S(1)}, bf16[2,1024,256]{2,1,0:T(8,128)(2,1)S(1)}, u32[]{:S(2)}, u32[]{:S(2)}) collective-permute-start(bf16[2,1024,256]{2,1,0:T(8,128)(2,1)S(1)} %maximum_select_fusion.2), channel_id=1, source_target_pairs={{0,8},{8,0},{1,9},{9,1},{2,10},{10,2},{3,11},{11,3},{4,12},{12,4},... | collective-permute-start | bytes 3145736 | tf_op jit(solution)/shard_map/ppermute | solution.py:18
  101.1 1.7 collective-permute-start.12
  102.8 2.1 collective-permute-done.13
  105.2 18.4 %collective-permute-done.9 = bf16[2,1024,256]{2,1,0:T(8,128)(2,1)S(1)} collective-permute-done((bf16[2,1024,256]{2,1,0:T(8,128)(2,1)S(1)}, bf16[2,1024,256]{2,1,0:T(8,128)(2,1)S(1)}, u32[]{:S(2)}, u32[]{:S(2)}) %collective-permute-start.9) | collective-permute-done | bytes 1048608 | tf_op jit(solution)/shard_map/ppermute | solution.py:18
  127.4 2.5 pad_maximum_fusion
  129.9 6.6 %reshape.1677 = f32[2,2,1024,256]{2,1,3,0:T(2,128)} reshape(f32[2,2048,256]{1,2,0:T(8,128)} %pad_maximum_fusion) | data formatting | bytes 8388608 | tf_op jit(solution)/shard_map/reshape | solution.py:137
  136.5 9.1 %fusion.211 = (f32[2,1,1024,256]{2,1,3,0:T(1,128)}, f32[2,1,1024,256]{2,1,3,0:T(1,128)}) fusion(f32[2,2,1024,256]{2,1,3,0:T(2,128)} %reshape.1677), kind=kLoop, calls=%fused_computation.412 | loop fusion | bytes 8388608 | tf_op jit(solution)/shard_map/slice | solution.py:139
  145.6 4.6 %copy.157 = f32[2,1,1024,256]{3,2,0,1:T(8,128)S(1)} copy(f32[2,1,1024,256]{2,1,3,0:T(1,128)} %get-tuple-element.141) | data formatting | bytes 4194304
  150.2 6.0 %copy.158 = f32[2,1,1024,256]{3,2,0,1:T(8,128)} copy(f32[2,1,1024,256]{2,1,3,0:T(1,128)} %get-tuple-element.142) | data formatting | bytes 4194304
  156.2 1.9 fusion.36
  158.3 3.1 %collective-permute-start.14 = (bf16[2,256,256]{2,1,0:T(8,128)(2,1)S(1)}, bf16[2,256,256]{2,1,0:T(8,128)(2,1)S(1)}, u32[]{:S(2)}, u32[]{:S(2)}) collective-permute-start(bf16[2,256,256]{2,1,0:T(8,128)(2,1)S(1)} %fusion.50), channel_id=1, source_target_pairs={{0,2},{2,0},{1,3},{3,1},{4,6},{6,4},{5,7},{7,5},{8,10},{10,8},{9,1... | collective-permute-start | bytes 786440 | tf_op jit(solution)/shard_map/ppermute | solution.py:18
  163.7 3.3 %collective-permute-done.14 = bf16[2,256,256]{2,1,0:T(8,128)(2,1)S(1)} collective-permute-done((bf16[2,256,256]{2,1,0:T(8,128)(2,1)S(1)}, bf16[2,256,256]{2,1,0:T(8,128)(2,1)S(1)}, u32[]{:S(2)}, u32[]{:S(2)}) %collective-permute-start.14) | collective-permute-done | bytes 262176 | tf_op jit(solution)/shard_map/ppermute | solution.py:18
  167.9 14.9 %collective-permute-done.16 = bf16[2,1024,256]{2,1,0:T(8,128)(2,1)S(1)} collective-permute-done((bf16[2,1024,256]{2,1,0:T(8,128)(2,1)S(1)}, bf16[2,1024,256]{2,1,0:T(8,128)(2,1)S(1)}, u32[]{:S(2)}, u32[]{:S(2)}) %collective-permute-start.16) | collective-permute-done | bytes 1048608 | tf_op jit(solution)/shard_map/ppermute | solution.py:18
  185.6 6.9 %collective-permute-done.17 = bf16[2,512,256]{2,1,0:T(8,128)(2,1)S(1)} collective-permute-done((bf16[2,512,256]{2,1,0:T(8,128)(2,1)S(1)}, bf16[2,512,256]{2,1,0:T(8,128)(2,1)S(1)}, u32[]{:S(2)}, u32[]{:S(2)}) %collective-permute-start.17) | collective-permute-done | bytes 524320 | tf_op jit(solution)/shard_map/ppermute | solution.py:18
  193.5 3.5 %collective-permute-start.18 = (bf16[2,256,256]{2,1,0:T(8,128)(2,1)}, bf16[2,256,256]{2,1,0:T(8,128)(2,1)S(1)}, u32[]{:S(2)}, u32[]{:S(2)}) collective-permute-start(bf16[2,256,256]{2,1,0:T(8,128)(2,1)} %fusion.51), channel_id=1, source_target_pairs={{0,2},{2,0},{1,3},{3,1},{4,6},{6,4},{5,7},{7,5},{8,10},{10,8},{9,1... | collective-permute-start | bytes 786440 | tf_op jit(solution)/shard_map/ppermute | solution.py:18
  199.1 63.0 %psum.7 = f32[256]{0:T(256)} all-reduce(f32[256]{0:T(256)S(1)} %bitcast.569), channel_id=1, replica_groups=mesh['dp'=8,'ctx'=16] {'dp','ctx'}, use_global_device_ids=true, to_apply=%region_1.2 | all-reduce | flops 256 | bytes 2048 | tf_op jit(solution)/shard_map/psum | solution.py:217
  264.4 3.2 %collective-permute-done.19 = bf16[2,128,256]{2,1,0:T(8,128)(2,1)S(1)} collective-permute-done((bf16[2,128,256]{2,1,0:T(8,128)(2,1)S(1)}, bf16[2,128,256]{2,1,0:T(8,128)(2,1)S(1)}, u32[]{:S(2)}, u32[]{:S(2)}) %collective-permute-start.19) | collective-permute-done | bytes 131104 | tf_op jit(solution)/shard_map/ppermute | solution.py:18
  267.9 2.4 fusion.3
  (328 shorter events, 69.6 us)
Async XLA Ops:
  5.4 26.5 %collective-permute-start = (bf16[2,128,256]{2,1,0:T(8,128)(2,1)S(1)}, bf16[2,128,256]{2,1,0:T(8,128)(2,1)S(1)}, u32[]{:S(2)}, u32[]{:S(2)}) collective-permute-start(bf16[2,128,256]{2,1,0:T(8,128)(2,1)S(1)} %bitcast_dynamic-update-slice_fusion.6), channel_id=1, source_target_pairs={{0,1},{1,0},{2,3},{3,2},{4,5},{5,4},{6,7},{7,6},{8,9},{9,8},{10,11... | collective-permute-start | bytes 393224 | tf_op jit(solution)/shard_map/ppermute | solution.py:18
  7.9 26.5 %collective-permute-start.1 = (bf16[2,128,256]{2,1,0:T(8,128)(2,1)S(1)}, bf16[2,128,256]{2,1,0:T(8,128)(2,1)S(1)}, u32[]{:S(2)}, u32[]{:S(2)}) collective-permute-start(bf16[2,128,256]{2,1,0:T(8,128)(2,1)S(1)} %bitcast_dynamic-update-slice_fusion.4), channel_id=1, source_target_pairs={{0,1},{1,0},{2,3},{3,2},{4,5},{5,4},{6,7},{7,6},{8,9},{9,8},{10,11... | collective-permute-start | bytes 393224 | tf_op jit(solution)/shard_map/ppermute | solution.py:18
  9.4 32.7 %collective-permute-start.3 = (bf16[2,128,256]{2,1,0:T(8,128)(2,1)S(1)}, bf16[2,128,256]{2,1,0:T(8,128)(2,1)S(1)}, u32[]{:S(2)}, u32[]{:S(2)}) collective-permute-start(bf16[2,128,256]{2,1,0:T(8,128)(2,1)S(1)} %bitcast_dynamic-update-slice_fusion.2), channel_id=1, source_target_pairs={{0,1},{1,0},{2,3},{3,2},{4,5},{5,4},{6,7},{7,6},{8,9},{9,8},{10,11... | collective-permute-start | bytes 393224 | tf_op jit(solution)/shard_map/ppermute | solution.py:18
  11.9 27.4 %collective-permute-start.6 = (bf16[2,128,256]{2,1,0:T(8,128)(2,1)S(1)}, bf16[2,128,256]{2,1,0:T(8,128)(2,1)S(1)}, u32[]{:S(2)}, u32[]{:S(2)}) collective-permute-start(bf16[2,128,256]{2,1,0:T(8,128)(2,1)S(1)} %bitcast_dynamic-update-slice_fusion), channel_id=1, source_target_pairs={{0,1},{1,0},{2,3},{3,2},{4,5},{5,4},{6,7},{7,6},{8,9},{9,8},{10,11... | collective-permute-start | bytes 393224 | tf_op jit(solution)/shard_map/ppermute | solution.py:18
  33.0 12.7 %copy-start.61 = (f32[2,1,128]{2,1,0:T(1,128)S(1)}, f32[2,1,128]{2,1,0:T(1,128)}, u32[]{:S(2)}) copy-start(f32[2,1,128]{2,1,0:T(1,128)} %fusion.187) | copy-start | bytes 3076
  34.6 10.8 %collective-permute-start.2 = (bf16[2,256,256]{2,1,0:T(8,128)(2,1)S(1)}, bf16[2,256,256]{2,1,0:T(8,128)(2,1)S(1)}, u32[]{:S(2)}, u32[]{:S(2)}) collective-permute-start(bf16[2,256,256]{2,1,0:T(8,128)(2,1)S(1)} %maximum_select_fusion.7), channel_id=1, source_target_pairs={{0,2},{2,0},{1,3},{3,1},{4,6},{6,4},{5,7},{7,5},{8,10},{10,8},{9,1... | collective-permute-start | bytes 786440 | tf_op jit(solution)/shard_map/ppermute | solution.py:18
  38.7 58.8 %collective-permute-start.10 = (bf16[2,128,256]{2,1,0:T(8,128)(2,1)}, bf16[2,128,256]{2,1,0:T(8,128)(2,1)}, u32[]{:S(2)}, u32[]{:S(2)}) collective-permute-start(bf16[2,128,256]{2,1,0:T(8,128)(2,1)} %fusion.67), channel_id=1, source_target_pairs={{0,1},{1,0},{2,3},{3,2},{4,5},{5,4},{6,7},{7,6},{8,9},{9,8},{10,11... | collective-permute-start | bytes 393224 | tf_op jit(solution)/shard_map/ppermute | solution.py:18
  40.1 26.1 %collective-permute-start.7 = (bf16[2,256,256]{2,1,0:T(8,128)(2,1)}, bf16[2,256,256]{2,1,0:T(8,128)(2,1)}, u32[]{:S(2)}, u32[]{:S(2)}) collective-permute-start(bf16[2,256,256]{2,1,0:T(8,128)(2,1)} %maximum_select_fusion.9), channel_id=1, source_target_pairs={{0,2},{2,0},{1,3},{3,1},{4,6},{6,4},{5,7},{7,5},{8,10},{10,8},{9,1... | collective-permute-start | bytes 786440 | tf_op jit(solution)/shard_map/ppermute | solution.py:18
  42.9 14.2 %collective-permute-start.4 = (bf16[2,256,256]{2,1,0:T(8,128)(2,1)}, bf16[2,256,256]{2,1,0:T(8,128)(2,1)}, u32[]{:S(2)}, u32[]{:S(2)}) collective-permute-start(bf16[2,256,256]{2,1,0:T(8,128)(2,1)} %maximum_select_fusion.8), channel_id=1, source_target_pairs={{0,2},{2,0},{1,3},{3,1},{4,6},{6,4},{5,7},{7,5},{8,10},{10,8},{9,1... | collective-permute-start | bytes 786440 | tf_op jit(solution)/shard_map/ppermute | solution.py:18
  58.4 14.8 %collective-permute-start.5 = (bf16[2,512,256]{2,1,0:T(8,128)(2,1)S(1)}, bf16[2,512,256]{2,1,0:T(8,128)(2,1)}, u32[]{:S(2)}, u32[]{:S(2)}) collective-permute-start(bf16[2,512,256]{2,1,0:T(8,128)(2,1)S(1)} %maximum_select_fusion.4), channel_id=1, source_target_pairs={{0,4},{4,0},{1,5},{5,1},{2,6},{6,2},{3,7},{7,3},{8,12},{12,8},{9,1... | collective-permute-start | bytes 1572872 | tf_op jit(solution)/shard_map/ppermute | solution.py:18
  62.3 12.3 %copy-start.19 = (bf16[2,1,16384]{2,0,1:T(2,128)(2,1)S(1)}, bf16[2,1,16384]{2,0,1:T(2,128)(2,1)}, u32[]{:S(2)}) copy-start(bf16[2,1,16384]{2,0,1:T(2,128)(2,1)} %copy.384) | copy-start | bytes 196612
  63.1 36.2 %collective-permute-start.11 = (bf16[2,256,256]{2,1,0:T(8,128)(2,1)}, bf16[2,256,256]{2,1,0:T(8,128)(2,1)}, u32[]{:S(2)}, u32[]{:S(2)}) collective-permute-start(bf16[2,256,256]{2,1,0:T(8,128)(2,1)} %fusion.49), channel_id=1, source_target_pairs={{0,2},{2,0},{1,3},{3,1},{4,6},{6,4},{5,7},{7,5},{8,10},{10,8},{9,1... | collective-permute-start | bytes 786440 | tf_op jit(solution)/shard_map/ppermute | solution.py:18
  68.3 23.8 %collective-permute-start.8 = (bf16[2,512,256]{2,1,0:T(8,128)(2,1)}, bf16[2,512,256]{2,1,0:T(8,128)(2,1)}, u32[]{:S(2)}, u32[]{:S(2)}) collective-permute-start(bf16[2,512,256]{2,1,0:T(8,128)(2,1)} %maximum_select_fusion.5), channel_id=1, source_target_pairs={{0,4},{4,0},{1,5},{5,1},{2,6},{6,2},{3,7},{7,3},{8,12},{12,8},{9,1... | collective-permute-start | bytes 1572872 | tf_op jit(solution)/shard_map/ppermute | solution.py:18
  89.4 15.5 %collective-permute-start.13 = (bf16[2,512,256]{2,1,0:T(8,128)(2,1)S(1)}, bf16[2,512,256]{2,1,0:T(8,128)(2,1)S(1)}, u32[]{:S(2)}, u32[]{:S(2)}) collective-permute-start(bf16[2,512,256]{2,1,0:T(8,128)(2,1)S(1)} %fusion.42), channel_id=1, source_target_pairs={{0,4},{4,0},{1,5},{5,1},{2,6},{6,2},{3,7},{7,3},{8,12},{12,8},{9,1... | collective-permute-start | bytes 1572872 | tf_op jit(solution)/shard_map/ppermute | solution.py:18
  93.8 29.7 %collective-permute-start.9 = (bf16[2,1024,256]{2,1,0:T(8,128)(2,1)S(1)}, bf16[2,1024,256]{2,1,0:T(8,128)(2,1)S(1)}, u32[]{:S(2)}, u32[]{:S(2)}) collective-permute-start(bf16[2,1024,256]{2,1,0:T(8,128)(2,1)S(1)} %maximum_select_fusion.2), channel_id=1, source_target_pairs={{0,8},{8,0},{1,9},{9,1},{2,10},{10,2},{3,11},{11,3},{4,12},{12,4},... | collective-permute-start | bytes 3145736 | tf_op jit(solution)/shard_map/ppermute | solution.py:18
  101.1 60.6 %collective-permute-start.12 = (bf16[2,128,256]{2,1,0:T(8,128)(2,1)}, bf16[2,128,256]{2,1,0:T(8,128)(2,1)}, u32[]{:S(2)}, u32[]{:S(2)}) collective-permute-start(bf16[2,128,256]{2,1,0:T(8,128)(2,1)} %fusion.68), channel_id=1, source_target_pairs={{0,1},{1,0},{2,3},{3,2},{4,5},{5,4},{6,7},{7,6},{8,9},{9,8},{10,11... | collective-permute-start | bytes 393224 | tf_op jit(solution)/shard_map/ppermute | solution.py:18
  105.1 19.0 %copy-start.18 = (bf16[2,1,16384]{2,0,1:T(2,128)(2,1)S(1)}, bf16[2,1,16384]{2,0,1:T(2,128)(2,1)}, u32[]{:S(2)}) copy-start(bf16[2,1,16384]{2,0,1:T(2,128)(2,1)} %copy.388) | copy-start | bytes 196612
  105.1 19.0 %copy-start.48 = (f32[2]{0:T(128)S(1)}, f32[2]{0:T(128)}, u32[]{:S(2)}) copy-start(f32[2]{0:T(128)} %copy-done.47) | copy-start | bytes 28
  105.2 19.0 %copy-start.59 = (f32[2,1,128]{2,1,0:T(1,128)S(1)}, f32[2,1,128]{2,1,0:T(1,128)}, u32[]{:S(2)}) copy-start(f32[2,1,128]{2,1,0:T(1,128)} %fusion.167) | copy-start | bytes 3076
  158.1 24.7 %collective-permute-start.16 = (bf16[2,1024,256]{2,1,0:T(8,128)(2,1)S(1)}, bf16[2,1024,256]{2,1,0:T(8,128)(2,1)S(1)}, u32[]{:S(2)}, u32[]{:S(2)}) collective-permute-start(bf16[2,1024,256]{2,1,0:T(8,128)(2,1)S(1)} %fusion.36), channel_id=1, source_target_pairs={{0,8},{8,0},{1,9},{9,1},{2,10},{10,2},{3,11},{11,3},{4,12},{12,4},... | collective-permute-start | bytes 3145736 | tf_op jit(solution)/shard_map/ppermute | solution.py:18
  158.3 8.7 %collective-permute-start.14 = (bf16[2,256,256]{2,1,0:T(8,128)(2,1)S(1)}, bf16[2,256,256]{2,1,0:T(8,128)(2,1)S(1)}, u32[]{:S(2)}, u32[]{:S(2)}) collective-permute-start(bf16[2,256,256]{2,1,0:T(8,128)(2,1)S(1)} %fusion.50), channel_id=1, source_target_pairs={{0,2},{2,0},{1,3},{3,1},{4,6},{6,4},{5,7},{7,5},{8,10},{10,8},{9,1... | collective-permute-start | bytes 786440 | tf_op jit(solution)/shard_map/ppermute | solution.py:18
  161.6 21.2 %copy-start = (f32[2,1,1024,256]{3,2,0,1:T(8,128)S(1)}, f32[2,1,1024,256]{3,2,0,1:T(8,128)}, u32[]{:S(2)}) copy-start(f32[2,1,1024,256]{3,2,0,1:T(8,128)} %copy.158) | copy-start | bytes 6291460
  167.1 16.3 %copy-start.12 = (bf16[2,1024,256]{2,1,0:T(8,128)(2,1)S(1)}, bf16[2,1024,256]{2,1,0:T(8,128)(2,1)}, u32[]{:S(2)}) copy-start(bf16[2,1024,256]{2,1,0:T(8,128)(2,1)} %copy-done.11) | copy-start | bytes 3145732
  167.1 16.3 %copy-start.16 = (bf16[2,128,1024]{2,1,0:T(8,128)(2,1)S(1)}, bf16[2,128,1024]{2,1,0:T(8,128)(2,1)}, u32[]{:S(2)}) copy-start(bf16[2,128,1024]{2,1,0:T(8,128)(2,1)} %copy-done.15) | copy-start | bytes 1572868
  167.1 16.7 %collective-permute-start.15 = (bf16[2,128,256]{2,1,0:T(8,128)(2,1)S(1)}, bf16[2,128,256]{2,1,0:T(8,128)(2,1)S(1)}, u32[]{:S(2)}, u32[]{:S(2)}) collective-permute-start(bf16[2,128,256]{2,1,0:T(8,128)(2,1)S(1)} %fusion.69), channel_id=1, source_target_pairs={{0,1},{1,0},{2,3},{3,2},{4,5},{5,4},{6,7},{7,6},{8,9},{9,8},{10,11... | collective-permute-start | bytes 393224 | tf_op jit(solution)/shard_map/ppermute | solution.py:18
  183.3 9.3 %collective-permute-start.17 = (bf16[2,512,256]{2,1,0:T(8,128)(2,1)S(1)}, bf16[2,512,256]{2,1,0:T(8,128)(2,1)S(1)}, u32[]{:S(2)}, u32[]{:S(2)}) collective-permute-start(bf16[2,512,256]{2,1,0:T(8,128)(2,1)S(1)} %fusion.43), channel_id=1, source_target_pairs={{0,4},{4,0},{1,5},{5,1},{2,6},{6,2},{3,7},{7,3},{8,12},{12,8},{9,1... | collective-permute-start | bytes 1572872 | tf_op jit(solution)/shard_map/ppermute | solution.py:18
  193.5 68.7 %collective-permute-start.18 = (bf16[2,256,256]{2,1,0:T(8,128)(2,1)}, bf16[2,256,256]{2,1,0:T(8,128)(2,1)S(1)}, u32[]{:S(2)}, u32[]{:S(2)}) collective-permute-start(bf16[2,256,256]{2,1,0:T(8,128)(2,1)} %fusion.51), channel_id=1, source_target_pairs={{0,2},{2,0},{1,3},{3,1},{4,6},{6,4},{5,7},{7,5},{8,10},{10,8},{9,1... | collective-permute-start | bytes 786440 | tf_op jit(solution)/shard_map/ppermute | solution.py:18
  198.3 65.4 %copy-start.37 = (f32[256]{0:T(256)S(1)}, f32[256]{0:T(256)}, u32[]{:S(2)}) copy-start(f32[256]{0:T(256)} %param.13) | copy-start | bytes 3076
  199.1 68.8 %copy-start.17 = (f32[2,2,32768]{2,1,0:T(2,128)S(1)}, f32[2,2,32768]{2,1,0:T(2,128)}, u32[]{:S(2)}) copy-start(f32[2,2,32768]{2,1,0:T(2,128)} %reshape.1667) | copy-start | bytes 1572868
  199.1 68.8 %copy-start.21 = (f32[1,2,128,256]{3,1,2,0:T(2,128)S(1)}, f32[1,2,128,256]{3,1,2,0:T(2,128)}, u32[]{:S(2)}) copy-start(f32[1,2,128,256]{3,1,2,0:T(2,128)} %copy.191) | copy-start | bytes 786436
  199.1 68.8 %copy-start.22 = (f32[1,2,128,256]{3,1,2,0:T(2,128)S(1)}, f32[1,2,128,256]{3,1,2,0:T(2,128)}, u32[]{:S(2)}) copy-start(f32[1,2,128,256]{3,1,2,0:T(2,128)} %copy.192) | copy-start | bytes 786436
  262.3 5.3 %collective-permute-start.19 = (bf16[2,128,256]{2,1,0:T(8,128)(2,1)S(1)}, bf16[2,128,256]{2,1,0:T(8,128)(2,1)S(1)}, u32[]{:S(2)}, u32[]{:S(2)}) collective-permute-start(bf16[2,128,256]{2,1,0:T(8,128)(2,1)S(1)} %fusion.70), channel_id=1, source_target_pairs={{0,1},{1,0},{2,3},{3,2},{4,5},{5,4},{6,7},{7,6},{8,9},{9,8},{10,11... | collective-permute-start | bytes 393224 | tf_op jit(solution)/shard_map/ppermute | solution.py:18
  (51 other events, 309.8 us)
where the time goes:
time: 277 us; the launch traced here: 273 us
  waiting for transfers between devices  63.6 us (23%)
  blocking collectives  63 us (23%)
  local copies, waits for them, and re-layouts  59.3 us (21%)
  starting transfers between devices  34.9 us (13%)
  other arithmetic  27.5 us (10%)
  matrix products  21.6 us (8%)
    ppermute x20, waiting for transfers between devices, swapped(): return lax.ppermute(block, axis, route)  63.6 us
    psum x1, blocking collectives, body(): lax.psum(jnp.sum(query_raw.astype(jnp.float32) * dq_rows, axis=0), ('dp',...  63 us
    ppermute x20, starting transfers between devices, swapped(): return lax.ppermute(block, axis, route)  34.9 us
    unnamed x153, local copies, waits for them, and re-layouts  24.8 us
    slice x3, local copies, waits for them, and re-layouts, swap_down(): kept_half = jnp.where(lower_half, halves[:, 0], halves[:, 1])  12.9 us
    reshape x3, local copies, waits for them, and re-layouts, swap_down(): halves = sums_kv.reshape(head_count, 2, -1, sums_kv.shape[-1])  10.3 us
    dot_general x25, matrix products, pick_blocks(): jnp.einsum('hsb,hbx->hsx', table, flat, precision=lax.Precision.HIGHEST,...  10.3 us
    select_n x10, other arithmetic, swap_up(): jnp.where(lower_half, jnp.concatenate([payload, partner], axis=1), jnp.co...  9.27 us
  transfers between devices with their start and end apart: 20, of which 9 were waited for; matrix products, arithmetic and copies ran while one was open for 34% of the time, Pallas kernels for 0%

commit v1 on v0

--- a/solution.py
+++ b/solution.py
@@ -6,6 +6,11 @@
 
 BLOCK = 128
 LEVELS = 5
+
+
+def one_after_other(x, first, second):
+    partial = lax.psum(x, first)
+    return lax.psum(partial, second)
 
 
 def swapped(block, axis, stride):
@@ -214,7 +219,9 @@
     grad_queries = (dq_rows * q_gain).astype(jnp.bfloat16)
     grad_keys = to_rows(kv_acc[..., :head_dim]).astype(jnp.bfloat16)
     grad_values = to_rows(kv_acc[..., head_dim:]).astype(jnp.bfloat16)
-    gain_total = lax.psum(jnp.sum(query_raw.astype(jnp.float32) * dq_rows, axis=0), ("dp", "ctx"))
+    gain_total = one_after_other(
+        jnp.sum(query_raw.astype(jnp.float32) * dq_rows, axis=0), "ctx", "dp"
+    )
     return (grad_queries[None], grad_keys[None], grad_values[None], gain_total)
 
 

time: 277 us -> 264 us (0.953)
  blocking collectives: 63 us -> 49.2 us
    psum x1 -> x2, blocking collectives: 63 us -> 49.2 us  [the longest x1 36.2 us: one_after_other(): partial = lax.psum(x, first)]
  transfers between devices with their start and end apart: 20 -> 20, of which waited for: 9 -> 9; matrix products, arithmetic and copies ran while one was open for 34% -> 36% of each run, Pallas kernels for 0% -> 0%
where the time goes in v1:
time: 264 us; the launch traced here: 259 us
  waiting for transfers between devices  63.5 us (24%)
  local copies, waits for them, and re-layouts  58.9 us (22%)
  blocking collectives  49.2 us (19%)
  starting transfers between devices  35.5 us (13%)
  other arithmetic  27.6 us (10%)
  matrix products  21.7 us (8%)
    ppermute x20, waiting for transfers between devices, swapped(): return lax.ppermute(block, axis, route)  63.5 us
    psum x1, blocking collectives, one_after_other(): partial = lax.psum(x, first)  36.2 us
    ppermute x20, starting transfers between devices, swapped(): return lax.ppermute(block, axis, route)  35.5 us
    unnamed x153, local copies, waits for them, and re-layouts  24.5 us
    psum x1, blocking collectives, one_after_other(): return lax.psum(partial, second)  13 us
    slice x3, local copies, waits for them, and re-layouts, swap_down(): kept_half = jnp.where(lower_half, halves[:, 0], halves[:, 1])  12.9 us
    dot_general x25, matrix products, pick_blocks(): jnp.einsum('hsb,hbx->hsx', table, flat, precision=lax.Precision.HIGHEST,...  10.3 us
    reshape x3, local copies, waits for them, and re-layouts, swap_down(): halves = sums_kv.reshape(head_count, 2, -1, sums_kv.shape[-1])  10.3 us
  transfers between devices with their start and end apart: 20, of which 9 were waited for; matrix products, arithmetic and copies ran while one was open for 36% of the time, Pallas kernels for 0%

profile of v1, /device:TPU:0, one launch (start us, length us, event | category | flops | bytes accessed | tf_op | source)
XLA Modules:
  0.0 259.1 jit_solution(16658535741942920779)
XLA Ops:
  1.7 1.7 clamp_reduce_fusion.3
  34.7 3.2 %collective-permute-start.2 = (bf16[2,256,256]{2,1,0:T(8,128)(2,1)S(1)}, bf16[2,256,256]{2,1,0:T(8,128)(2,1)S(1)}, u32[]{:S(2)}, u32[]{:S(2)}) collective-permute-start(bf16[2,256,256]{2,1,0:T(8,128)(2,1)S(1)} %maximum_select_fusion.7), channel_id=1, source_target_pairs={{0,2},{2,0},{1,3},{3,1},{4,6},{6,4},{5,7},{7,5},{8,10},{10,8},{9,1... | collective-permute-start | bytes 786440 | tf_op jit(solution)/shard_map/ppermute | solution.py:23
  40.3 2.0 collective-permute-start.7
  48.1 9.2 %collective-permute-done.4 = bf16[2,256,256]{2,1,0:T(8,128)(2,1)} collective-permute-done((bf16[2,256,256]{2,1,0:T(8,128)(2,1)}, bf16[2,256,256]{2,1,0:T(8,128)(2,1)}, u32[]{:S(2)}, u32[]{:S(2)}) %collective-permute-start.4) | collective-permute-done | bytes 262176 | tf_op jit(solution)/shard_map/ppermute | solution.py:23
  58.6 2.4 collective-permute-start.5
  63.3 3.0 %collective-permute-start.11 = (bf16[2,256,256]{2,1,0:T(8,128)(2,1)}, bf16[2,256,256]{2,1,0:T(8,128)(2,1)}, u32[]{:S(2)}, u32[]{:S(2)}) collective-permute-start(bf16[2,256,256]{2,1,0:T(8,128)(2,1)} %fusion.49), channel_id=1, source_target_pairs={{0,2},{2,0},{1,3},{3,1},{4,6},{6,4},{5,7},{7,5},{8,10},{10,8},{9,1... | collective-permute-start | bytes 786440 | tf_op jit(solution)/shard_map/ppermute | solution.py:23
  66.3 2.1 maximum_select_fusion.5
  68.6 4.8 %collective-permute-done.5 = bf16[2,512,256]{2,1,0:T(8,128)(2,1)} collective-permute-done((bf16[2,512,256]{2,1,0:T(8,128)(2,1)S(1)}, bf16[2,512,256]{2,1,0:T(8,128)(2,1)}, u32[]{:S(2)}, u32[]{:S(2)}) %collective-permute-start.5) | collective-permute-done | bytes 524320 | tf_op jit(solution)/shard_map/ppermute | solution.py:23
  78.7 3.0 %reshape.1673 = f32[2,2,512,256]{2,1,3,0:T(2,128)S(1)} reshape(f32[2,1024,256]{1,2,0:T(8,128)} %pad_maximum_fusion.1) | data formatting | bytes 4194304 | tf_op jit(solution)/shard_map/reshape | solution.py:142
  81.7 3.0 %fusion.212 = (f32[2,1,512,256]{2,1,3,0:T(1,128)}, f32[2,1,512,256]{2,1,3,0:T(1,128)}) fusion(f32[2,2,512,256]{2,1,3,0:T(2,128)S(1)} %reshape.1673), kind=kLoop, calls=%fused_computation.413 | loop fusion | bytes 4194304 | tf_op jit(solution)/shard_map/slice | solution.py:144
  84.7 2.3 copy.151
  87.1 2.4 copy.152
  89.6 2.7 %collective-permute-start.13 = (bf16[2,512,256]{2,1,0:T(8,128)(2,1)S(1)}, bf16[2,512,256]{2,1,0:T(8,128)(2,1)S(1)}, u32[]{:S(2)}, u32[]{:S(2)}) collective-permute-start(bf16[2,512,256]{2,1,0:T(8,128)(2,1)S(1)} %fusion.42), channel_id=1, source_target_pairs={{0,4},{4,0},{1,5},{5,1},{2,6},{6,2},{3,7},{7,3},{8,12},{12,8},{9,1... | collective-permute-start | bytes 1572872 | tf_op jit(solution)/shard_map/ppermute | solution.py:23
  92.3 1.8 maximum_select_fusion.2
  94.0 3.7 %collective-permute-start.9 = (bf16[2,1024,256]{2,1,0:T(8,128)(2,1)S(1)}, bf16[2,1024,256]{2,1,0:T(8,128)(2,1)S(1)}, u32[]{:S(2)}, u32[]{:S(2)}) collective-permute-start(bf16[2,1024,256]{2,1,0:T(8,128)(2,1)S(1)} %maximum_select_fusion.2), channel_id=1, source_target_pairs={{0,8},{8,0},{1,9},{9,1},{2,10},{10,2},{3,11},{11,3},{4,12},{12,4},... | collective-permute-start | bytes 3145736 | tf_op jit(solution)/shard_map/ppermute | solution.py:23
  103.1 2.0 collective-permute-done.13
  105.4 18.4 %collective-permute-done.9 = bf16[2,1024,256]{2,1,0:T(8,128)(2,1)S(1)} collective-permute-done((bf16[2,1024,256]{2,1,0:T(8,128)(2,1)S(1)}, bf16[2,1024,256]{2,1,0:T(8,128)(2,1)S(1)}, u32[]{:S(2)}, u32[]{:S(2)}) %collective-permute-start.9) | collective-permute-done | bytes 1048608 | tf_op jit(solution)/shard_map/ppermute | solution.py:23
  127.6 2.5 pad_maximum_fusion
  130.1 6.6 %reshape.1677 = f32[2,2,1024,256]{2,1,3,0:T(2,128)} reshape(f32[2,2048,256]{1,2,0:T(8,128)} %pad_maximum_fusion) | data formatting | bytes 8388608 | tf_op jit(solution)/shard_map/reshape | solution.py:142
  136.7 9.1 %fusion.211 = (f32[2,1,1024,256]{2,1,3,0:T(1,128)}, f32[2,1,1024,256]{2,1,3,0:T(1,128)}) fusion(f32[2,2,1024,256]{2,1,3,0:T(2,128)} %reshape.1677), kind=kLoop, calls=%fused_computation.412 | loop fusion | bytes 8388608 | tf_op jit(solution)/shard_map/slice | solution.py:144
  145.8 4.6 %copy.157 = f32[2,1,1024,256]{3,2,0,1:T(8,128)S(1)} copy(f32[2,1,1024,256]{2,1,3,0:T(1,128)} %get-tuple-element.141) | data formatting | bytes 4194304
  150.4 6.1 %copy.158 = f32[2,1,1024,256]{3,2,0,1:T(8,128)} copy(f32[2,1,1024,256]{2,1,3,0:T(1,128)} %get-tuple-element.142) | data formatting | bytes 4194304
  156.4 1.9 fusion.36
  158.5 3.1 %collective-permute-start.14 = (bf16[2,256,256]{2,1,0:T(8,128)(2,1)S(1)}, bf16[2,256,256]{2,1,0:T(8,128)(2,1)S(1)}, u32[]{:S(2)}, u32[]{:S(2)}) collective-permute-start(bf16[2,256,256]{2,1,0:T(8,128)(2,1)S(1)} %fusion.50), channel_id=1, source_target_pairs={{0,2},{2,0},{1,3},{3,1},{4,6},{6,4},{5,7},{7,5},{8,10},{10,8},{9,1... | collective-permute-start | bytes 786440 | tf_op jit(solution)/shard_map/ppermute | solution.py:23
  164.0 3.3 %collective-permute-done.14 = bf16[2,256,256]{2,1,0:T(8,128)(2,1)S(1)} collective-permute-done((bf16[2,256,256]{2,1,0:T(8,128)(2,1)S(1)}, bf16[2,256,256]{2,1,0:T(8,128)(2,1)S(1)}, u32[]{:S(2)}, u32[]{:S(2)}) %collective-permute-start.14) | collective-permute-done | bytes 262176 | tf_op jit(solution)/shard_map/ppermute | solution.py:23
  168.2 14.6 %collective-permute-done.16 = bf16[2,1024,256]{2,1,0:T(8,128)(2,1)S(1)} collective-permute-done((bf16[2,1024,256]{2,1,0:T(8,128)(2,1)S(1)}, bf16[2,1024,256]{2,1,0:T(8,128)(2,1)S(1)}, u32[]{:S(2)}, u32[]{:S(2)}) %collective-permute-start.16) | collective-permute-done | bytes 1048608 | tf_op jit(solution)/shard_map/ppermute | solution.py:23
  185.7 6.9 %collective-permute-done.17 = bf16[2,512,256]{2,1,0:T(8,128)(2,1)S(1)} collective-permute-done((bf16[2,512,256]{2,1,0:T(8,128)(2,1)S(1)}, bf16[2,512,256]{2,1,0:T(8,128)(2,1)S(1)}, u32[]{:S(2)}, u32[]{:S(2)}) %collective-permute-start.17) | collective-permute-done | bytes 524320 | tf_op jit(solution)/shard_map/ppermute | solution.py:23
  193.5 3.8 %collective-permute-start.18 = (bf16[2,256,256]{2,1,0:T(8,128)(2,1)}, bf16[2,256,256]{2,1,0:T(8,128)(2,1)S(1)}, u32[]{:S(2)}, u32[]{:S(2)}) collective-permute-start(bf16[2,256,256]{2,1,0:T(8,128)(2,1)} %fusion.51), channel_id=1, source_target_pairs={{0,2},{2,0},{1,3},{3,1},{4,6},{6,4},{5,7},{7,5},{8,10},{10,8},{9,1... | collective-permute-start | bytes 786440 | tf_op jit(solution)/shard_map/ppermute | solution.py:23
  199.4 36.2 %psum.14 = f32[256]{0:T(256)S(1)} all-reduce(f32[256]{0:T(256)S(1)} %bitcast.569), channel_id=1, replica_groups=mesh['dp'=8,'ctx'=16] {'ctx'}, use_global_device_ids=true, to_apply=%region_1.2 | all-reduce | flops 256 | bytes 2048 | tf_op jit(solution)/shard_map/psum | solution.py:12
  235.6 13.0 %psum.15 = f32[256]{0:T(256)} all-reduce(f32[256]{0:T(256)S(1)} %psum.14), channel_id=1, replica_groups=mesh['dp'=8,'ctx'=16] {'dp'}, use_global_device_ids=true, to_apply=%region_2.3 | all-reduce | flops 256 | bytes 2048 | tf_op jit(solution)/shard_map/psum | solution.py:13
  250.8 3.4 %collective-permute-done.19 = bf16[2,128,256]{2,1,0:T(8,128)(2,1)S(1)} collective-permute-done((bf16[2,128,256]{2,1,0:T(8,128)(2,1)S(1)}, bf16[2,128,256]{2,1,0:T(8,128)(2,1)S(1)}, u32[]{:S(2)}, u32[]{:S(2)}) %collective-permute-start.19) | collective-permute-done | bytes 131104 | tf_op jit(solution)/shard_map/ppermute | solution.py:23
  254.5 2.4 fusion.3
  (329 shorter events, 71.5 us)
Async XLA Ops:
  5.4 26.6 %collective-permute-start = (bf16[2,128,256]{2,1,0:T(8,128)(2,1)S(1)}, bf16[2,128,256]{2,1,0:T(8,128)(2,1)S(1)}, u32[]{:S(2)}, u32[]{:S(2)}) collective-permute-start(bf16[2,128,256]{2,1,0:T(8,128)(2,1)S(1)} %bitcast_dynamic-update-slice_fusion.6), channel_id=1, source_target_pairs={{0,1},{1,0},{2,3},{3,2},{4,5},{5,4},{6,7},{7,6},{8,9},{9,8},{10,11... | collective-permute-start | bytes 393224 | tf_op jit(solution)/shard_map/ppermute | solution.py:23
  7.9 26.7 %collective-permute-start.1 = (bf16[2,128,256]{2,1,0:T(8,128)(2,1)S(1)}, bf16[2,128,256]{2,1,0:T(8,128)(2,1)S(1)}, u32[]{:S(2)}, u32[]{:S(2)}) collective-permute-start(bf16[2,128,256]{2,1,0:T(8,128)(2,1)S(1)} %bitcast_dynamic-update-slice_fusion.4), channel_id=1, source_target_pairs={{0,1},{1,0},{2,3},{3,2},{4,5},{5,4},{6,7},{7,6},{8,9},{9,8},{10,11... | collective-permute-start | bytes 393224 | tf_op jit(solution)/shard_map/ppermute | solution.py:23
  9.4 32.8 %collective-permute-start.3 = (bf16[2,128,256]{2,1,0:T(8,128)(2,1)S(1)}, bf16[2,128,256]{2,1,0:T(8,128)(2,1)S(1)}, u32[]{:S(2)}, u32[]{:S(2)}) collective-permute-start(bf16[2,128,256]{2,1,0:T(8,128)(2,1)S(1)} %bitcast_dynamic-update-slice_fusion.2), channel_id=1, source_target_pairs={{0,1},{1,0},{2,3},{3,2},{4,5},{5,4},{6,7},{7,6},{8,9},{9,8},{10,11... | collective-permute-start | bytes 393224 | tf_op jit(solution)/shard_map/ppermute | solution.py:23
  11.9 27.5 %collective-permute-start.6 = (bf16[2,128,256]{2,1,0:T(8,128)(2,1)S(1)}, bf16[2,128,256]{2,1,0:T(8,128)(2,1)S(1)}, u32[]{:S(2)}, u32[]{:S(2)}) collective-permute-start(bf16[2,128,256]{2,1,0:T(8,128)(2,1)S(1)} %bitcast_dynamic-update-slice_fusion), channel_id=1, source_target_pairs={{0,1},{1,0},{2,3},{3,2},{4,5},{5,4},{6,7},{7,6},{8,9},{9,8},{10,11... | collective-permute-start | bytes 393224 | tf_op jit(solution)/shard_map/ppermute | solution.py:23
  33.1 12.7 %copy-start.61 = (f32[2,1,128]{2,1,0:T(1,128)S(1)}, f32[2,1,128]{2,1,0:T(1,128)}, u32[]{:S(2)}) copy-start(f32[2,1,128]{2,1,0:T(1,128)} %fusion.187) | copy-start | bytes 3076
  34.7 10.9 %collective-permute-start.2 = (bf16[2,256,256]{2,1,0:T(8,128)(2,1)S(1)}, bf16[2,256,256]{2,1,0:T(8,128)(2,1)S(1)}, u32[]{:S(2)}, u32[]{:S(2)}) collective-permute-start(bf16[2,256,256]{2,1,0:T(8,128)(2,1)S(1)} %maximum_select_fusion.7), channel_id=1, source_target_pairs={{0,2},{2,0},{1,3},{3,1},{4,6},{6,4},{5,7},{7,5},{8,10},{10,8},{9,1... | collective-permute-start | bytes 786440 | tf_op jit(solution)/shard_map/ppermute | solution.py:23
  38.9 58.9 %collective-permute-start.10 = (bf16[2,128,256]{2,1,0:T(8,128)(2,1)}, bf16[2,128,256]{2,1,0:T(8,128)(2,1)}, u32[]{:S(2)}, u32[]{:S(2)}) collective-permute-start(bf16[2,128,256]{2,1,0:T(8,128)(2,1)} %fusion.67), channel_id=1, source_target_pairs={{0,1},{1,0},{2,3},{3,2},{4,5},{5,4},{6,7},{7,6},{8,9},{9,8},{10,11... | collective-permute-start | bytes 393224 | tf_op jit(solution)/shard_map/ppermute | solution.py:23
  40.3 26.1 %collective-permute-start.7 = (bf16[2,256,256]{2,1,0:T(8,128)(2,1)}, bf16[2,256,256]{2,1,0:T(8,128)(2,1)}, u32[]{:S(2)}, u32[]{:S(2)}) collective-permute-start(bf16[2,256,256]{2,1,0:T(8,128)(2,1)} %maximum_select_fusion.9), channel_id=1, source_target_pairs={{0,2},{2,0},{1,3},{3,1},{4,6},{6,4},{5,7},{7,5},{8,10},{10,8},{9,1... | collective-permute-start | bytes 786440 | tf_op jit(solution)/shard_map/ppermute | solution.py:23
  43.1 14.2 %collective-permute-start.4 = (bf16[2,256,256]{2,1,0:T(8,128)(2,1)}, bf16[2,256,256]{2,1,0:T(8,128)(2,1)}, u32[]{:S(2)}, u32[]{:S(2)}) collective-permute-start(bf16[2,256,256]{2,1,0:T(8,128)(2,1)} %maximum_select_fusion.8), channel_id=1, source_target_pairs={{0,2},{2,0},{1,3},{3,1},{4,6},{6,4},{5,7},{7,5},{8,10},{10,8},{9,1... | collective-permute-start | bytes 786440 | tf_op jit(solution)/shard_map/ppermute | solution.py:23
  58.6 14.8 %collective-permute-start.5 = (bf16[2,512,256]{2,1,0:T(8,128)(2,1)S(1)}, bf16[2,512,256]{2,1,0:T(8,128)(2,1)}, u32[]{:S(2)}, u32[]{:S(2)}) collective-permute-start(bf16[2,512,256]{2,1,0:T(8,128)(2,1)S(1)} %maximum_select_fusion.4), channel_id=1, source_target_pairs={{0,4},{4,0},{1,5},{5,1},{2,6},{6,2},{3,7},{7,3},{8,12},{12,8},{9,1... | collective-permute-start | bytes 1572872 | tf_op jit(solution)/shard_map/ppermute | solution.py:23
  62.5 12.3 %copy-start.19 = (bf16[2,1,16384]{2,0,1:T(2,128)(2,1)S(1)}, bf16[2,1,16384]{2,0,1:T(2,128)(2,1)}, u32[]{:S(2)}) copy-start(bf16[2,1,16384]{2,0,1:T(2,128)(2,1)} %copy.384) | copy-start | bytes 196612
  63.3 36.3 %collective-permute-start.11 = (bf16[2,256,256]{2,1,0:T(8,128)(2,1)}, bf16[2,256,256]{2,1,0:T(8,128)(2,1)}, u32[]{:S(2)}, u32[]{:S(2)}) collective-permute-start(bf16[2,256,256]{2,1,0:T(8,128)(2,1)} %fusion.49), channel_id=1, source_target_pairs={{0,2},{2,0},{1,3},{3,1},{4,6},{6,4},{5,7},{7,5},{8,10},{10,8},{9,1... | collective-permute-start | bytes 786440 | tf_op jit(solution)/shard_map/ppermute | solution.py:23
  68.5 23.8 %collective-permute-start.8 = (bf16[2,512,256]{2,1,0:T(8,128)(2,1)}, bf16[2,512,256]{2,1,0:T(8,128)(2,1)}, u32[]{:S(2)}, u32[]{:S(2)}) collective-permute-start(bf16[2,512,256]{2,1,0:T(8,128)(2,1)} %maximum_select_fusion.5), channel_id=1, source_target_pairs={{0,4},{4,0},{1,5},{5,1},{2,6},{6,2},{3,7},{7,3},{8,12},{12,8},{9,1... | collective-permute-start | bytes 1572872 | tf_op jit(solution)/shard_map/ppermute | solution.py:23
  89.6 15.5 %collective-permute-start.13 = (bf16[2,512,256]{2,1,0:T(8,128)(2,1)S(1)}, bf16[2,512,256]{2,1,0:T(8,128)(2,1)S(1)}, u32[]{:S(2)}, u32[]{:S(2)}) collective-permute-start(bf16[2,512,256]{2,1,0:T(8,128)(2,1)S(1)} %fusion.42), channel_id=1, source_target_pairs={{0,4},{4,0},{1,5},{5,1},{2,6},{6,2},{3,7},{7,3},{8,12},{12,8},{9,1... | collective-permute-start | bytes 1572872 | tf_op jit(solution)/shard_map/ppermute | solution.py:23
  94.0 29.7 %collective-permute-start.9 = (bf16[2,1024,256]{2,1,0:T(8,128)(2,1)S(1)}, bf16[2,1024,256]{2,1,0:T(8,128)(2,1)S(1)}, u32[]{:S(2)}, u32[]{:S(2)}) collective-permute-start(bf16[2,1024,256]{2,1,0:T(8,128)(2,1)S(1)} %maximum_select_fusion.2), channel_id=1, source_target_pairs={{0,8},{8,0},{1,9},{9,1},{2,10},{10,2},{3,11},{11,3},{4,12},{12,4},... | collective-permute-start | bytes 3145736 | tf_op jit(solution)/shard_map/ppermute | solution.py:23
  101.4 60.6 %collective-permute-start.12 = (bf16[2,128,256]{2,1,0:T(8,128)(2,1)}, bf16[2,128,256]{2,1,0:T(8,128)(2,1)}, u32[]{:S(2)}, u32[]{:S(2)}) collective-permute-start(bf16[2,128,256]{2,1,0:T(8,128)(2,1)} %fusion.68), channel_id=1, source_target_pairs={{0,1},{1,0},{2,3},{3,2},{4,5},{5,4},{6,7},{7,6},{8,9},{9,8},{10,11... | collective-permute-start | bytes 393224 | tf_op jit(solution)/shard_map/ppermute | solution.py:23
  105.3 19.0 %copy-start.18 = (bf16[2,1,16384]{2,0,1:T(2,128)(2,1)S(1)}, bf16[2,1,16384]{2,0,1:T(2,128)(2,1)}, u32[]{:S(2)}) copy-start(bf16[2,1,16384]{2,0,1:T(2,128)(2,1)} %copy.388) | copy-start | bytes 196612
  105.3 19.0 %copy-start.48 = (f32[2]{0:T(128)S(1)}, f32[2]{0:T(128)}, u32[]{:S(2)}) copy-start(f32[2]{0:T(128)} %copy-done.47) | copy-start | bytes 28
  105.4 19.0 %copy-start.59 = (f32[2,1,128]{2,1,0:T(1,128)S(1)}, f32[2,1,128]{2,1,0:T(1,128)}, u32[]{:S(2)}) copy-start(f32[2,1,128]{2,1,0:T(1,128)} %fusion.167) | copy-start | bytes 3076
  158.3 24.5 %collective-permute-start.16 = (bf16[2,1024,256]{2,1,0:T(8,128)(2,1)S(1)}, bf16[2,1024,256]{2,1,0:T(8,128)(2,1)S(1)}, u32[]{:S(2)}, u32[]{:S(2)}) collective-permute-start(bf16[2,1024,256]{2,1,0:T(8,128)(2,1)S(1)} %fusion.36), channel_id=1, source_target_pairs={{0,8},{8,0},{1,9},{9,1},{2,10},{10,2},{3,11},{11,3},{4,12},{12,4},... | collective-permute-start | bytes 3145736 | tf_op jit(solution)/shard_map/ppermute | solution.py:23
  158.5 8.8 %collective-permute-start.14 = (bf16[2,256,256]{2,1,0:T(8,128)(2,1)S(1)}, bf16[2,256,256]{2,1,0:T(8,128)(2,1)S(1)}, u32[]{:S(2)}, u32[]{:S(2)}) collective-permute-start(bf16[2,256,256]{2,1,0:T(8,128)(2,1)S(1)} %fusion.50), channel_id=1, source_target_pairs={{0,2},{2,0},{1,3},{3,1},{4,6},{6,4},{5,7},{7,5},{8,10},{10,8},{9,1... | collective-permute-start | bytes 786440 | tf_op jit(solution)/shard_map/ppermute | solution.py:23
  161.8 21.0 %copy-start = (f32[2,1,1024,256]{3,2,0,1:T(8,128)S(1)}, f32[2,1,1024,256]{3,2,0,1:T(8,128)}, u32[]{:S(2)}) copy-start(f32[2,1,1024,256]{3,2,0,1:T(8,128)} %copy.158) | copy-start | bytes 6291460
  167.4 16.4 %copy-start.12 = (bf16[2,1024,256]{2,1,0:T(8,128)(2,1)S(1)}, bf16[2,1024,256]{2,1,0:T(8,128)(2,1)}, u32[]{:S(2)}) copy-start(bf16[2,1024,256]{2,1,0:T(8,128)(2,1)} %copy-done.11) | copy-start | bytes 3145732
  167.4 16.4 %copy-start.16 = (bf16[2,128,1024]{2,1,0:T(8,128)(2,1)S(1)}, bf16[2,128,1024]{2,1,0:T(8,128)(2,1)}, u32[]{:S(2)}) copy-start(bf16[2,128,1024]{2,1,0:T(8,128)(2,1)} %copy-done.15) | copy-start | bytes 1572868
  167.4 16.8 %collective-permute-start.15 = (bf16[2,128,256]{2,1,0:T(8,128)(2,1)S(1)}, bf16[2,128,256]{2,1,0:T(8,128)(2,1)S(1)}, u32[]{:S(2)}, u32[]{:S(2)}) collective-permute-start(bf16[2,128,256]{2,1,0:T(8,128)(2,1)S(1)} %fusion.69), channel_id=1, source_target_pairs={{0,1},{1,0},{2,3},{3,2},{4,5},{5,4},{6,7},{7,6},{8,9},{9,8},{10,11... | collective-permute-start | bytes 393224 | tf_op jit(solution)/shard_map/ppermute | solution.py:23
  183.3 9.3 %collective-permute-start.17 = (bf16[2,512,256]{2,1,0:T(8,128)(2,1)S(1)}, bf16[2,512,256]{2,1,0:T(8,128)(2,1)S(1)}, u32[]{:S(2)}, u32[]{:S(2)}) collective-permute-start(bf16[2,512,256]{2,1,0:T(8,128)(2,1)S(1)} %fusion.43), channel_id=1, source_target_pairs={{0,4},{4,0},{1,5},{5,1},{2,6},{6,2},{3,7},{7,3},{8,12},{12,8},{9,1... | collective-permute-start | bytes 1572872 | tf_op jit(solution)/shard_map/ppermute | solution.py:23
  193.5 55.0 %collective-permute-start.18 = (bf16[2,256,256]{2,1,0:T(8,128)(2,1)}, bf16[2,256,256]{2,1,0:T(8,128)(2,1)S(1)}, u32[]{:S(2)}, u32[]{:S(2)}) collective-permute-start(bf16[2,256,256]{2,1,0:T(8,128)(2,1)} %fusion.51), channel_id=1, source_target_pairs={{0,2},{2,0},{1,3},{3,1},{4,6},{6,4},{5,7},{7,5},{8,10},{10,8},{9,1... | collective-permute-start | bytes 786440 | tf_op jit(solution)/shard_map/ppermute | solution.py:23
  198.6 51.5 %copy-start.37 = (f32[256]{0:T(256)S(1)}, f32[256]{0:T(256)}, u32[]{:S(2)}) copy-start(f32[256]{0:T(256)} %param.13) | copy-start | bytes 3076
  199.3 55.1 %copy-start.17 = (f32[2,2,32768]{2,1,0:T(2,128)S(1)}, f32[2,2,32768]{2,1,0:T(2,128)}, u32[]{:S(2)}) copy-start(f32[2,2,32768]{2,1,0:T(2,128)} %reshape.1667) | copy-start | bytes 1572868
  199.3 55.1 %copy-start.21 = (f32[1,2,128,256]{3,1,2,0:T(2,128)S(1)}, f32[1,2,128,256]{3,1,2,0:T(2,128)}, u32[]{:S(2)}) copy-start(f32[1,2,128,256]{3,1,2,0:T(2,128)} %copy.191) | copy-start | bytes 786436
  199.3 55.1 %copy-start.22 = (f32[1,2,128,256]{3,1,2,0:T(2,128)S(1)}, f32[1,2,128,256]{3,1,2,0:T(2,128)}, u32[]{:S(2)}) copy-start(f32[1,2,128,256]{3,1,2,0:T(2,128)} %copy.192) | copy-start | bytes 786436
  248.7 5.5 %collective-permute-start.19 = (bf16[2,128,256]{2,1,0:T(8,128)(2,1)S(1)}, bf16[2,128,256]{2,1,0:T(8,128)(2,1)S(1)}, u32[]{:S(2)}, u32[]{:S(2)}) collective-permute-start(bf16[2,128,256]{2,1,0:T(8,128)(2,1)S(1)} %fusion.70), channel_id=1, source_target_pairs={{0,1},{1,0},{2,3},{3,2},{4,5},{5,4},{6,7},{7,6},{8,9},{9,8},{10,11... | collective-permute-start | bytes 393224 | tf_op jit(solution)/shard_map/ppermute | solution.py:23
  (51 other events, 312.8 us)
